TPU v7x, 32 devices: a whole 2x2x4 slice. The times are simulated.
32 devices in a mesh: rows: 16 (over z, y, core), cols: 2 (over x).
Axes of the slice: x: 2, y: 2, z: 4, core: 2. Of those that a mesh axis runs over, the one named last changes fastest.
Arguments:
- sketch: bfloat16 [128, 32768], P('cols', 'rows'), may hold values from -6 to 6
- geometry: float32 [3, 32768], P(None, 'rows'), may hold values from 0 to 32, as said below
- neighbours: int32 [32, 5], replicated, may hold values from 0 to 31, as said below
- counts: int32 [32], replicated, may hold values from 1 to 5, as said below
Outputs:
- modes: float32 [128, 32768], P('cols', 'rows')
Inputs may be any that keep to these rules, and one draw needn't show every extreme that they name: `geometry`: row 0 of block b lies in [b, b + 1); row 1 lies in [0, 16); row 2 is positive. `neighbours`: in row r the first counts[r] entries are distinct blocks c with |c - r| <= 2, r itself among them; the remaining entries equal r. `counts`: some row block has all 5 column blocks.
All inputs are finite; a program needn't handle non-finite values.
Results may differ from a plain program's by a relative error of at most 0.0059.
Values may be sent and summed in bfloat16 or wider, within the bound.
A program may use at most 64 MiB of HBM per device.

v0:
```python
import functools
import math

import jax
import jax.numpy as jnp
from jax import lax
from jax.experimental import pallas as pl
from jax.experimental.pallas import tpu as pltpu
from jax.sharding import PartitionSpec as P

B = 1024
BLK_DEV = 2


highest = lax.Precision.HIGHEST


def padded(shard, sides, width):
    for axis, dim in sides:
        size, length = (lax.axis_size(axis), shard.shape[dim])
        up = [(i, (i + 1) % size) for i in range(size - 1)]
        down = [(j, i) for i, j in up]
        last = lax.slice_in_dim(shard, length - width, length, axis=dim)
        initial = lax.slice_in_dim(shard, 0, width, axis=dim)
        before = lax.ppermute(last, axis, up)
        after = lax.ppermute(initial, axis, down)
        shard = jnp.concatenate([before, shard, after], axis=dim)
    return shard


def spread(value, axis, source):
    kept = jnp.where(lax.axis_index(axis) == source, value, 0).astype(value.dtype)
    return lax.psum(kept, axis)


def kernel_tile(col_geo, row_geo, wavenumber):
    delta_x = col_geo[0][:, None] - row_geo[0][None, :]
    delta_y = col_geo[1][:, None] - row_geo[1][None, :]
    distance = jnp.sqrt(delta_x * delta_x + delta_y * delta_y)
    weights = col_geo[2][:, None] * row_geo[2][None, :]
    return (weights * jnp.sinc(distance * (wavenumber / math.pi))).astype(jnp.bfloat16)


def choose_slice(own_array, start, width):
    own_part = lax.dynamic_slice_in_dim(own_array, start, width, 1)
    return own_part


def task_lists(neighbours, counts, device_index, unit_blocks):
    slot_count = neighbours.shape[1]
    unit_count = unit_blocks.shape[0]
    slot_ids = jnp.arange(slot_count, dtype=jnp.int32)
    owners = jnp.zeros((unit_count,), jnp.int32) + device_index
    row_blocks = owners * BLK_DEV + unit_blocks
    flags = (slot_ids[None, :] < counts[row_blocks][:, None]).astype(jnp.int32).reshape(-1)
    column_ids = neighbours[row_blocks].reshape(-1)
    base_blocks = jnp.repeat(owners * BLK_DEV - BLK_DEV, slot_count)
    starts = (column_ids - base_blocks) * B
    task_total = flags.shape[0]
    task_ids = jnp.arange(task_total, dtype=jnp.int32)
    rank = jnp.cumsum(flags) - flags
    taken = flags == 1
    task_sides = jnp.zeros((task_total,), jnp.int32)
    target = jnp.where(taken, rank, task_total)
    blank = jnp.zeros((task_total + 1,), jnp.int32)
    order_side = blank.at[target].set(task_sides)
    order_unit = blank.at[target].set(task_ids // slot_count % unit_count)
    order_start = blank.at[target].set(starts)
    return (order_side, order_unit, order_start, jnp.sum(taken.astype(jnp.int32)))


def evaluate_tiles(tables, geo_wide, unit_blocks, unit_offset, unit_rows, capacity, wavenumber):
    order_side, order_unit, order_start, own_count = tables

    def add_tile(task, stored):
        row_start = (BLK_DEV + unit_blocks[order_unit[task]]) * B + unit_offset
        row_geo = choose_slice(geo_wide, row_start, unit_rows)
        col_geo = choose_slice(geo_wide, order_start[task], B)
        tile = kernel_tile(col_geo, row_geo, wavenumber)
        return lax.dynamic_update_slice(stored, tile[None], (task, 0, 0))

    initial = jnp.zeros((capacity, B, unit_rows), jnp.bfloat16)
    return lax.fori_loop(0, own_count, add_tile, initial)


def apply_tiles(stored, tables, panel_wide, unit_rows, unit_count):
    order_side, order_unit, order_start, own_count = tables
    columns = panel_wide.shape[0]
    side_count = 1

    def add_term(task, running):
        col_panel = choose_slice(panel_wide, order_start[task], B)
        term = jnp.dot(col_panel, stored[task], preferred_element_type=jnp.float32)
        return running + term[None]

    initial = jnp.zeros((side_count, columns, unit_count * unit_rows), jnp.float32)
    return lax.fori_loop(0, own_count, add_term, initial)


def operator_product(panel_t, stored, tables, unit_rows, unit_count):
    panel_wide = padded(panel_t, (("rows", 1),), BLK_DEV * B)
    gathered = apply_tiles(
        stored,
        tables,
        lax.all_gather(panel_wide, "cols", axis=0, tiled=True),
        unit_rows,
        unit_count,
    )[0]
    return lax.all_to_all(gathered, "cols", split_axis=0, concat_axis=1, tiled=True)


def normalize(current):
    gram_matrix = lax.psum(jnp.dot(current, current.T, precision=highest), "rows")
    cholesky_factor = jnp.linalg.cholesky(gram_matrix)
    return lax.linalg.triangular_solve(cholesky_factor, current, left_side=True, lower=True)


def orthonormal(second_product):
    position = lax.axis_index("cols")
    panels = lax.axis_size("cols")
    norm_scale = math.sqrt(second_product.shape[1] * lax.axis_size("rows"))
    mode_rows = jnp.zeros_like(second_product)
    removed = jnp.zeros_like(second_product)
    for panel_index in range(panels):
        basis_rows = normalize(second_product - removed)
        mode_rows = jnp.where(position == panel_index, basis_rows, mode_rows)
        if panel_index + 1 < panels:
            finished = spread(basis_rows, "cols", panel_index)
            coefficients = lax.psum(jnp.dot(finished, second_product.T, precision=highest), "rows")
            update = jnp.dot(coefficients.T, finished, precision=highest)
            removed = removed + jnp.where(position > panel_index, update, 0.0)
    return mode_rows * norm_scale


def body(sketch, geometry, neighbours, counts):
    wavenumber = 4.0 * math.sqrt(B)
    device_index = lax.axis_index("rows")
    geo_wide = padded(geometry, (("rows", 1),), BLK_DEV * B)
    unit_blocks = jnp.arange(BLK_DEV, dtype=jnp.int32)
    unit_offset = 0
    unit_rows = BLK_DEV * B // lax.axis_size("cols")
    slice_start = lax.axis_index("cols") * unit_rows
    unit_blocks = jnp.reshape(slice_start // B, (1,))
    unit_offset = slice_start % B
    unit_count = unit_blocks.shape[0]
    tables = task_lists(neighbours, counts, device_index, unit_blocks)
    capacity = unit_count * neighbours.shape[1]
    stored = evaluate_tiles(
        tables, geo_wide, unit_blocks, unit_offset, unit_rows, capacity, wavenumber
    )
    first_product = operator_product(sketch, stored, tables, unit_rows, unit_count).astype(
        jnp.bfloat16
    )
    second_product = operator_product(first_product, stored, tables, unit_rows, unit_count)
    return orthonormal(second_product)


MESH = pl.DeviceIdType.MESH
SLOTS = 5
CHUNK = 256
GROUP = 256
SIN = (
    6.28318330620465,
    -41.34144799998349,
    81.59666336606338,
    -76.58390226519525,
    41.21913554078422,
    -12.289783804974757,
)
MAGIC = 12582912.0


def column_range(dq, to_col):
    first = -2 * dq - to_col + 2
    kept = [e for e in range(2) if 0 <= first + e < SLOTS]
    lo, count = kept[0], len(kept)
    return (first + lo) * B, lo * B, count * B


def fast_kernel(
    rows_n,
    wavenumber,
    sketch,
    geometry,
    neighbours,
    counts,
    gram,
    second,
    tiles,
    wide,
    geo,
    weight,
    first,
    own_x,
    own_y,
    own_a,
    gram_send,
    gram_recv,
    geo_sem,
    sk_sem,
    first_sem,
    gram_sem,
    pair_sem,
):
    q = lax.axis_index("rows")
    x = lax.axis_index("cols")
    r = 2 * q + x
    blocks_n = 2 * rows_n
    flips = [1 << k for k in range(rows_n.bit_length() - 1)]

    def partner_q(flip):
        return q + flip - 2 * flip * ((q // flip) % 2)

    barrier = pltpu.get_barrier_semaphore()
    pl.semaphore_signal(barrier, inc=1, device_id=(q, 1 - x), device_id_type=MESH)
    for flip in flips[1:]:
        pl.semaphore_signal(barrier, inc=1, device_id=(partner_q(flip), x), device_id_type=MESH)
    for dq in (-1, 1):

        @pl.when((q + dq >= 0) & (q + dq < rows_n))
        def _(dq=dq):
            for c in range(2):
                pl.semaphore_signal(barrier, inc=1, device_id=(q + dq, c), device_id_type=MESH)

    for c in range(2):

        @pl.when(x == c)
        def _(c=c):
            at, _lo, _n = column_range(0, c)
            geo[:, at : at + 2 * B] = geometry[...]
            wide[64 * c : 64 * c + 64, at : at + 2 * B] = sketch[...]

    for step in (-2, -1, 1, 2):

        @pl.when((r + step < 0) | (r + step >= blocks_n))
        def _(step=step):
            at = (2 + step) * B
            geo[:, at : at + B] = jnp.full((3, B), -1.0, jnp.float32)
            wide[:, at : at + B] = jnp.zeros((128, B), jnp.bfloat16)
            first[at : at + B, :] = jnp.zeros((B, 128), jnp.bfloat16)

    sides = jnp.where(q > 0, 2, 0) + jnp.where(q < rows_n - 1, 2, 0)
    pl.semaphore_wait(barrier, len(flips) + sides)

    def geo_copy(dq, col):
        to, lo, n = column_range(dq, col)
        k = (dq + 1) // 2
        return pltpu.make_async_remote_copy(
            src_ref=geometry.at[:, lo : lo + n],
            dst_ref=geo.at[:, to : to + n],
            send_sem=geo_sem.at[0, k],
            recv_sem=geo_sem.at[1, k],
            device_id=(q + dq, x),
            device_id_type=MESH,
        )

    def sketch_copy(dq, from_col, to_col):
        to, lo, n = column_range(dq, to_col)
        k = (dq + 1) * 2 + (1 if from_col != to_col else 0)
        return pltpu.make_async_remote_copy(
            src_ref=sketch.at[:, lo : lo + n],
            dst_ref=wide.at[64 * from_col : 64 * from_col + 64, to : to + n],
            send_sem=sk_sem.at[0, k],
            recv_sem=sk_sem.at[1, k],
            device_id=(q + dq, to_col),
            device_id_type=MESH,
        )

    def inside(dq):
        return (q + dq >= 0) & (q + dq < rows_n)

    for c in range(2):
        for dq in (-1, 1):

            @pl.when((x == c) & inside(dq))
            def _(c=c, dq=dq):
                geo_copy(dq, c).start()

    for c in range(2):
        for dq in (-1, 0, 1):
            for to in range(2):
                if dq == 0 and to == c:
                    continue

                @pl.when((x == c) & inside(dq))
                def _(c=c, dq=dq, to=to):
                    sketch_copy(dq, c, to).start()

    to_turns = wavenumber / (2.0 * math.pi)

    def scale_window(at):
        base = (r - 2).astype(jnp.float32)
        weight[0:1, at] = (geo[0:1, at] - base) * to_turns
        weight[1:2, at] = geo[1:2, at] * to_turns

    scale_window(slice(2 * B, 3 * B))
    weight[2:3, 2 * B : 3 * B] = geo[2:3, 2 * B : 3 * B]

    def spread_own(i, carry):
        cols = pl.ds(pl.multiple_of(2 * B + i * 128, 128), 128)
        at = pl.ds(pl.multiple_of(i * 128, 128), 128)
        for row, ref in ((0, own_x), (1, own_y), (2, own_a)):
            line = jnp.broadcast_to(weight[row : row + 1, cols], (128, 128))
            ref[at, :] = jnp.transpose(line)
        return carry

    lax.fori_loop(0, B // 128, spread_own, 0)

    def wait_geo():
        for c in range(2):
            for dq in (-1, 1):

                @pl.when((x == c) & inside(-dq))
                def _(c=c, dq=dq):
                    geo_copy(dq, c).wait_recv()

    def mask_weights():
        for slot in range(SLOTS):
            hit = jnp.float32(0.0)
            for s in range(SLOTS):
                found = (neighbours[s, r] == r + slot - 2) & (s < counts[r])
                hit = jnp.maximum(hit, jnp.where(found, jnp.float32(1.0), jnp.float32(0.0)))
            at = slice(slot * B, slot * B + B)
            scale_window(at)
            weight[2:3, at] = geo[2:3, at] * (hit * (0.5 / math.pi))

    tiny = 2.5e-10

    def evaluate(i):
        def one(g, carry, width=GROUP):
            cols = pl.ds(pl.multiple_of(g * width, width), width)
            col_x, col_y, col_a = weight[0:1, cols], weight[1:2, cols], weight[2:3, cols]
            for h in range(CHUNK // 128):
                at = pl.ds(pl.multiple_of(i * CHUNK + h * 128, 128), 128)
                for lane in range(width // 128):
                    part = slice(lane * 128, lane * 128 + 128)
                    dx = own_x[at, :] - col_x[:, part]
                    dy = own_y[at, :] - col_y[:, part]
                    square = jnp.maximum(dx * dx + dy * dy, tiny)
                    inv = lax.rsqrt(square)
                    turns = square * inv
                    f = turns - ((turns + MAGIC) - MAGIC)
                    z = f * f
                    poly = jnp.float32(SIN[5])
                    for coefficient in SIN[4::-1]:
                        poly = poly * z + coefficient
                    value = (poly * f) * inv * (own_a[at, :] * col_a[:, part])
                    lanes = pl.ds(pl.multiple_of(g * width + lane * 128, 128), 128)
                    tiles[at, lanes] = value.astype(jnp.bfloat16)
            return carry

        per_block = B // GROUP

        def outside(g, carry):
            return one(jnp.where(g < 2, g, g + 1), carry, B)

        lax.fori_loop(0, 4, outside, 0)
        lax.fori_loop(2 * per_block + i, 3 * per_block, one, 0)

        def mirror(g, carry):
            at = pl.ds(pl.multiple_of(i * CHUNK, CHUNK), CHUNK)
            rows = pl.ds(pl.multiple_of(g * CHUNK, CHUNK), CHUNK)
            to = pl.ds(pl.multiple_of(2 * B + g * CHUNK, CHUNK), CHUNK)
            cols = pl.ds(pl.multiple_of(2 * B + i * CHUNK, CHUNK), CHUNK)
            tiles[at, to] = jnp.transpose(tiles[rows, cols])
            return carry

        lax.fori_loop(0, i, mirror, 0)

    steps = (-2, -1, 1, 2)

    def first_copy(i, k):
        target = r + steps[k]
        rows = pl.ds(pl.multiple_of(2 * B + i * CHUNK, CHUNK), CHUNK)
        to = pl.ds(pl.multiple_of((2 - steps[k]) * B + i * CHUNK, CHUNK), CHUNK)
        return pltpu.make_async_remote_copy(
            src_ref=first.at[rows, :],
            dst_ref=first.at[to, :],
            send_sem=first_sem.at[0, k, i],
            recv_sem=first_sem.at[1, k, i],
            device_id=(target // 2, target % 2),
            device_id_type=MESH,
        )

    def product_and_send(i):
        at = pl.ds(pl.multiple_of(i * CHUNK, CHUNK), CHUNK)
        part = lax.dot_general(
            tiles[at, :],
            wide[...],
            (((1,), (1,)), ((), ())),
            preferred_element_type=jnp.float32,
        )
        rows = pl.ds(pl.multiple_of(2 * B + i * CHUNK, CHUNK), CHUNK)
        first[rows, :] = part.astype(jnp.bfloat16)
        for k in range(4):

            @pl.when((r + steps[k] >= 0) & (r + steps[k] < blocks_n))
            def _(k=k):
                first_copy(i, k).start()

    wait_geo()
    mask_weights()
    chunks = B // CHUNK
    early = chunks // 2

    def eval_only(i, carry):
        evaluate(i)
        return carry

    lax.fori_loop(0, early, eval_only, 0)

    for c in range(2):
        for dq in (-1, 0, 1):
            for source in range(2):
                if dq == 0 and source == c:
                    continue

                @pl.when((x == c) & inside(-dq))
                def _(c=c, dq=dq, source=source):
                    sketch_copy(dq, source, c).wait_recv()

    def product_only(i, carry):
        product_and_send(i)
        return carry

    lax.fori_loop(0, early, product_only, 0)

    def both(i, carry):
        evaluate(i)
        product_and_send(i)
        return carry

    lax.fori_loop(early, chunks, both, 0)

    def first_wait(i, carry):
        for k in range(4):

            @pl.when((r - steps[k] >= 0) & (r - steps[k] < blocks_n))
            def _(k=k):
                first_copy(i, k).wait_recv()

            @pl.when((r + steps[k] >= 0) & (r + steps[k] < blocks_n))
            def _(k=k):
                first_copy(i, k).wait_send()

        return carry

    lax.fori_loop(0, chunks, first_wait, 0)

    def second_product(i, carry):
        at = pl.ds(pl.multiple_of(i * CHUNK, CHUNK), CHUNK)
        to = pl.ds(pl.multiple_of(x * B + i * CHUNK, CHUNK), CHUNK)
        part = jnp.dot(tiles[at, :], first[...], preferred_element_type=jnp.float32)
        second[to, :] = part
        turned = jnp.transpose(part)
        product = jnp.dot(
            turned, part, precision=lax.Precision.HIGHEST, preferred_element_type=jnp.float32
        )
        gram_send[0] += product
        return carry

    gram_send[0] = jnp.zeros((128, 128), jnp.float32)
    lax.fori_loop(0, chunks, second_product, 0)

    half = pl.ds(pl.multiple_of(x * B, B), B)
    pair = pltpu.make_async_remote_copy(
        src_ref=second.at[half, :],
        dst_ref=second.at[half, :],
        send_sem=pair_sem.at[0],
        recv_sem=pair_sem.at[1],
        device_id=(q, 1 - x),
        device_id_type=MESH,
    )

    targets = [(q, 1 - x)] + [(partner_q(flip), x) for flip in flips]
    for k, target in enumerate(targets):
        copy = pltpu.make_async_remote_copy(
            src_ref=gram_send.at[k],
            dst_ref=gram_recv.at[k],
            send_sem=gram_sem.at[0, k],
            recv_sem=gram_sem.at[1, k],
            device_id=target,
            device_id_type=MESH,
        )
        copy.start()
        if k == 0:
            pair.start()
        copy.wait()
        total = gram_send[k] + gram_recv[k]
        if k + 1 < len(targets):
            gram_send[k + 1] = total
        else:
            gram[...] = total

    for c in range(2):
        for dq in (-1, 1):

            @pl.when((x == c) & inside(dq))
            def _(c=c, dq=dq):
                geo_copy(dq, c).wait_send()

    for c in range(2):
        for dq in (-1, 0, 1):
            for to in range(2):
                if dq == 0 and to == c:
                    continue

                @pl.when((x == c) & inside(dq))
                def _(c=c, dq=dq, to=to):
                    sketch_copy(dq, c, to).wait_send()

    pair.wait()


def finish_kernel(scale, gram, second, modes, inverse):
    size = gram.shape[0]
    lane = lax.broadcasted_iota(jnp.int32, (8, size), 1)
    sub = lax.broadcasted_iota(jnp.int32, (8, size), 0)
    groups = [gram[8 * k : 8 * k + 8, :] for k in range(size // 8)]
    for j in range(size):
        own, inner = j // 8, j % 8
        line = groups[own][inner : inner + 1, :]
        root = lax.rsqrt(line[:, j : j + 1])
        line = jnp.where(lane[0:1] == j, 1.0, line) * root
        for k in range(own, size // 8):
            old = groups[k]
            column = old[:, j : j + 1] * root
            new = jnp.where(lane == j, 0.0, old) - column * line
            if k == own:
                new = jnp.where(sub > inner, new, jnp.where(sub == inner, line, old))
            groups[k] = new
    for k in range(size // 8):
        inverse[8 * k : 8 * k + 8, :] = jnp.where(lane <= sub + 8 * k, groups[k], 0.0) * scale
    start = pl.multiple_of(lax.axis_index("cols") * 64, 64)
    lower = inverse[pl.ds(start, 64), :]
    for i in range(4):
        at = slice(i * 512, i * 512 + 512)
        modes[:, at] = jnp.dot(
            lower,
            jnp.transpose(second[at, :]),
            precision=lax.Precision.HIGHEST,
            preferred_element_type=jnp.float32,
        )


def fast_body(sketch, geometry, neighbours, counts):
    rows_n = lax.axis_size("rows")
    wavenumber = 4.0 * math.sqrt(B)
    levels = 1 + rows_n.bit_length() - 1
    vmem = pl.BlockSpec(memory_space=pltpu.VMEM)
    smem = pl.BlockSpec(memory_space=pltpu.SMEM)
    gram, second = pl.pallas_call(
        functools.partial(fast_kernel, rows_n, wavenumber),
        name="sketch_twice",
        out_shape=(
            jax.ShapeDtypeStruct((128, 128), jnp.float32),
            jax.ShapeDtypeStruct((2 * B, 128), jnp.float32),
        ),
        in_specs=[vmem, vmem, smem, smem],
        out_specs=(vmem, vmem),
        scratch_shapes=[
            pltpu.VMEM((B, SLOTS * B), jnp.bfloat16),
            pltpu.VMEM((128, SLOTS * B), jnp.bfloat16),
            pltpu.VMEM((3, SLOTS * B), jnp.float32),
            pltpu.VMEM((3, SLOTS * B), jnp.float32),
            pltpu.VMEM((SLOTS * B, 128), jnp.bfloat16),
            pltpu.VMEM((B, 128), jnp.float32),
            pltpu.VMEM((B, 128), jnp.float32),
            pltpu.VMEM((B, 128), jnp.float32),
            pltpu.VMEM((levels, 128, 128), jnp.float32),
            pltpu.VMEM((levels, 128, 128), jnp.float32),
            pltpu.SemaphoreType.DMA((2, 2)),
            pltpu.SemaphoreType.DMA((2, 6)),
            pltpu.SemaphoreType.DMA((2, 4, B // CHUNK)),
            pltpu.SemaphoreType.DMA((2, levels)),
            pltpu.SemaphoreType.DMA((2,)),
        ],
        compiler_params=pltpu.CompilerParams(
            collective_id=0, has_side_effects=True, vmem_limit_bytes=48 * 1024 * 1024
        ),
    )(sketch, geometry, jnp.transpose(neighbours), counts)
    scale = math.sqrt(2 * B * rows_n)
    return pl.pallas_call(
        functools.partial(finish_kernel, scale),
        name="orthonormal_rows",
        out_shape=jax.ShapeDtypeStruct((64, 2 * B), jnp.float32),
        in_specs=[vmem, vmem],
        out_specs=vmem,
        scratch_shapes=[pltpu.VMEM((128, 128), jnp.float32)],
        compiler_params=pltpu.CompilerParams(vmem_limit_bytes=16 * 1024 * 1024),
    )(gram, second)


def solution(mesh):
    rows_n, cols_n = mesh.shape["rows"], mesh.shape["cols"]
    pair = cols_n == 2 and rows_n & (rows_n - 1) == 0
    return jax.shard_map(
        fast_body if pair else body,
        mesh=mesh,
        in_specs=(P("cols", "rows"), P(None, "rows"), P(), P()),
        out_specs=P("cols", "rows"),
        check_vma=False,
    )
```

profile of v0, /device:TPU:0, one launch (start us, length us, event | category | flops | bytes accessed | tf_op | source)
XLA Modules:
  0.0 74.6 jit_solution(2300534793549507187)
XLA Ops:
  0.0 0.0 copy-start.3
  0.0 0.7 copy-done.3
  0.7 0.0 copy-start
  0.7 0.9 %copy-done = bf16[64,2048]{1,0:T(8,128)(2,1)S(1)} copy-done((bf16[64,2048]{1,0:T(8,128)(2,1)S(1)}, bf16[64,2048]{1,0:T(8,128)(2,1)}, u32[]{:S(2)}) %copy-start) | copy-done | bytes 262168
  1.6 0.0 copy-start.1
  1.6 0.8 %copy-done.1 = f32[3,2048]{1,0:T(4,128)S(1)} copy-done((f32[3,2048]{1,0:T(4,128)S(1)}, f32[3,2048]{1,0:T(4,128)}, u32[]{:S(2)}) %copy-start.1) | copy-done | bytes 24600
  2.4 0.0 copy-start.2
  2.4 0.7 copy-done.2
  3.1 58.9 %sketch_twice.1 = (f32[128,128]{1,0:T(8,128)S(1)}, f32[2048,128]{1,0:T(8,128)S(1)}) custom-call(bf16[64,2048]{1,0:T(8,128)(2,1)S(1)} %copy-done, f32[3,2048]{1,0:T(4,128)S(1)} %copy-done.1, s32[5,32]{1,0:T(8,128)S(1)} %bitcast.1, s32[32]{0:T(128)S(1)} %copy-done.3), custom_call_target="tpu_custom_call" | custom-call | tf_op jit(solution)/shard_map/sketch_twice/pallas_call | solution.py:552
  62.0 12.7 %orthonormal_rows.1 = f32[64,2048]{1,0:T(8,128)} custom-call(f32[128,128]{1,0:T(8,128)S(1)} %get-tuple-element.7.gram, f32[2048,128]{1,0:T(8,128)S(1)} %get-tuple-element.8.second), custom_call_target="tpu_custom_call" | custom-call | tf_op jit(solution)/shard_map/orthonormal_rows/pallas_call | solution.py:583
Async XLA Ops:
  0.0 0.7 copy-start.3
  0.7 0.9 %copy-start = (bf16[64,2048]{1,0:T(8,128)(2,1)S(1)}, bf16[64,2048]{1,0:T(8,128)(2,1)}, u32[]{:S(2)}) copy-start(bf16[64,2048]{1,0:T(8,128)(2,1)} %sketch.1) | copy-start | bytes 786436
  1.6 0.8 %copy-start.1 = (f32[3,2048]{1,0:T(4,128)S(1)}, f32[3,2048]{1,0:T(4,128)}, u32[]{:S(2)}) copy-start(f32[3,2048]{1,0:T(4,128)} %geometry.1) | copy-start | bytes 73732
  2.4 0.7 copy-start.2
where the time goes:
time: 74.9 us; the launch traced here: 74.6 us
  Pallas kernels  71.6 us (96%)
  local copies, waits for them, and re-layouts  3.05 us (4%)
    pallas_call x1, Pallas kernels, fast_body(): pl.pallas_call(functools.partial(fast_kernel, rows_n, wavenumber), name='...  58.9 us
    pallas_call x1, Pallas kernels, fast_body(): pl.pallas_call(functools.partial(finish_kernel, scale), name='orthonormal...  12.7 us
    unnamed x8, local copies, waits for them, and re-layouts  3.05 us

commit v1 on v0

--- a/solution.py
+++ b/solution.py
@@ -182,8 +182,8 @@
     wavenumber,
     sketch,
     geometry,
-    neighbours,
-    counts,
+    neighbours_hbm,
+    counts_hbm,
     gram,
     second,
     tiles,
@@ -201,6 +201,9 @@
     first_sem,
     gram_sem,
     pair_sem,
+    local_sem,
+    neighbours,
+    counts,
 ):
     q = lax.axis_index("rows")
     x = lax.axis_index("cols")
@@ -219,16 +222,27 @@
 
         @pl.when((q + dq >= 0) & (q + dq < rows_n))
         def _(dq=dq):
-            for c in range(2):
-                pl.semaphore_signal(barrier, inc=1, device_id=(q + dq, c), device_id_type=MESH)
-
+            pl.semaphore_signal(barrier, inc=1, device_id=(q + dq, x), device_id_type=MESH)
+
+    def local_copy(c, k):
+        at = column_range(0, c)[0]
+        if k == 0:
+            return pltpu.make_async_copy(geometry, geo.at[:, at : at + 2 * B], local_sem.at[0])
+        held = wide.at[64 * c : 64 * c + 64, at : at + 2 * B]
+        return pltpu.make_async_copy(sketch, held, local_sem.at[1])
+
+    table_copies = (
+        pltpu.make_async_copy(neighbours_hbm, neighbours, local_sem.at[2]),
+        pltpu.make_async_copy(counts_hbm, counts, local_sem.at[3]),
+    )
+    for copy in table_copies:
+        copy.start()
     for c in range(2):
 
         @pl.when(x == c)
         def _(c=c):
-            at, _lo, _n = column_range(0, c)
-            geo[:, at : at + 2 * B] = geometry[...]
-            wide[64 * c : 64 * c + 64, at : at + 2 * B] = sketch[...]
+            local_copy(c, 0).start()
+            local_copy(c, 1).start()
 
     for step in (-2, -1, 1, 2):
 
@@ -239,7 +253,7 @@
             wide[:, at : at + B] = jnp.zeros((128, B), jnp.bfloat16)
             first[at : at + B, :] = jnp.zeros((B, 128), jnp.bfloat16)
 
-    sides = jnp.where(q > 0, 2, 0) + jnp.where(q < rows_n - 1, 2, 0)
+    sides = jnp.where(q > 0, 1, 0) + jnp.where(q < rows_n - 1, 1, 0)
     pl.semaphore_wait(barrier, len(flips) + sides)
 
     def geo_copy(dq, col):
@@ -254,15 +268,29 @@
             device_id_type=MESH,
         )
 
-    def sketch_copy(dq, from_col, to_col):
-        to, lo, n = column_range(dq, to_col)
-        k = (dq + 1) * 2 + (1 if from_col != to_col else 0)
+    def cross_copy(c):
+        at = column_range(0, 1 - c)[0]
         return pltpu.make_async_remote_copy(
-            src_ref=sketch.at[:, lo : lo + n],
-            dst_ref=wide.at[64 * from_col : 64 * from_col + 64, to : to + n],
+            src_ref=sketch,
+            dst_ref=wide.at[64 * c : 64 * c + 64, at : at + 2 * B],
+            send_sem=sk_sem.at[0, 0],
+            recv_sem=sk_sem.at[1, 0],
+            device_id=(q, 1 - c),
+            device_id_type=MESH,
+        )
+
+    def side_copy(dq, c, passed_on):
+        to, lo, n = column_range(dq, c)
+        k = (1 if dq < 0 else 2) + (2 if passed_on else 0)
+        panel = 1 - c if passed_on else c
+        lines = slice(64 * panel, 64 * panel + 64)
+        at = column_range(0, c)[0] + lo
+        return pltpu.make_async_remote_copy(
+            src_ref=wide.at[lines, at : at + n] if passed_on else sketch.at[:, lo : lo + n],
+            dst_ref=wide.at[lines, to : to + n],
             send_sem=sk_sem.at[0, k],
             recv_sem=sk_sem.at[1, k],
-            device_id=(q + dq, to_col),
+            device_id=(q + dq, c),
             device_id_type=MESH,
         )
 
@@ -277,14 +305,35 @@
                 geo_copy(dq, c).start()
 
     for c in range(2):
-        for dq in (-1, 0, 1):
-            for to in range(2):
-                if dq == 0 and to == c:
-                    continue
+
+        @pl.when(x == c)
+        def _(c=c):
+            cross_copy(c).start()
+
+        for dq in (-1, 1):
+
+            @pl.when((x == c) & inside(dq))
+            def _(c=c, dq=dq):
+                side_copy(dq, c, False).start()
+
+    def pass_sketch_on():
+        for c in range(2):
+
+            @pl.when(x == c)
+            def _(c=c):
+                cross_copy(1 - c).wait_recv()
+
+            for dq in (-1, 1):
 
                 @pl.when((x == c) & inside(dq))
-                def _(c=c, dq=dq, to=to):
-                    sketch_copy(dq, c, to).start()
+                def _(c=c, dq=dq):
+                    side_copy(dq, c, True).start()
+
+    for c in range(2):
+
+        @pl.when(x == c)
+        def _(c=c):
+            local_copy(c, 0).wait()
 
     to_turns = wavenumber / (2.0 * math.pi)
 
@@ -367,20 +416,38 @@
 
         lax.fori_loop(0, i, mirror, 0)
 
-    steps = (-2, -1, 1, 2)
+    onward = 1 - 2 * x
 
     def first_copy(i, k):
-        target = r + steps[k]
-        rows = pl.ds(pl.multiple_of(2 * B + i * CHUNK, CHUNK), CHUNK)
-        to = pl.ds(pl.multiple_of((2 - steps[k]) * B + i * CHUNK, CHUNK), CHUNK)
+        held = (2, 2, 2, 3 - 2 * x)[k]
+        slot = (4, 0, 1 + 2 * x, 1 + 2 * x)[k]
+        target = ((q - 1, x), (q + 1, x), (q, 1 - x), (q + onward, x))[k]
+        rows = pl.ds(pl.multiple_of(held * B + i * CHUNK, CHUNK), CHUNK)
+        to = pl.ds(pl.multiple_of(slot * B + i * CHUNK, CHUNK), CHUNK)
         return pltpu.make_async_remote_copy(
             src_ref=first.at[rows, :],
             dst_ref=first.at[to, :],
             send_sem=first_sem.at[0, k, i],
             recv_sem=first_sem.at[1, k, i],
-            device_id=(target // 2, target % 2),
+            device_id=target,
             device_id_type=MESH,
         )
+
+    def sends(k):
+        return (q > 0, q < rows_n - 1, None, inside(onward))[k]
+
+    def receives(k):
+        return (q < rows_n - 1, q > 0, None, inside(-onward))[k]
+
+    def guarded(condition, action):
+        if condition is None:
+            action()
+        else:
+            pl.when(condition)(action)
+
+    def pass_first_on(i):
+        first_copy(i, 2).wait_recv()
+        guarded(sends(3), lambda: first_copy(i, 3).start())
 
     def product_and_send(i):
         at = pl.ds(pl.multiple_of(i * CHUNK, CHUNK), CHUNK)
@@ -392,32 +459,36 @@
         )
         rows = pl.ds(pl.multiple_of(2 * B + i * CHUNK, CHUNK), CHUNK)
         first[rows, :] = part.astype(jnp.bfloat16)
-        for k in range(4):
-
-            @pl.when((r + steps[k] >= 0) & (r + steps[k] < blocks_n))
-            def _(k=k):
-                first_copy(i, k).start()
+        for k in (2, 0, 1):
+            guarded(sends(k), lambda k=k: first_copy(i, k).start())
 
     wait_geo()
+    for copy in table_copies:
+        copy.wait()
     mask_weights()
     chunks = B // CHUNK
-    early = chunks // 2
+    early = chunks - 1
 
     def eval_only(i, carry):
         evaluate(i)
         return carry
 
-    lax.fori_loop(0, early, eval_only, 0)
+    lax.fori_loop(0, 1, eval_only, 0)
+    pass_sketch_on()
+    lax.fori_loop(1, early, eval_only, 0)
 
     for c in range(2):
-        for dq in (-1, 0, 1):
-            for source in range(2):
-                if dq == 0 and source == c:
-                    continue
-
-                @pl.when((x == c) & inside(-dq))
-                def _(c=c, dq=dq, source=source):
-                    sketch_copy(dq, source, c).wait_recv()
+
+        @pl.when(x == c)
+        def _(c=c):
+            local_copy(c, 1).wait()
+
+        for dq in (-1, 1):
+
+            @pl.when((x == c) & inside(-dq))
+            def _(c=c, dq=dq):
+                side_copy(dq, c, False).wait_recv()
+                side_copy(dq, c, True).wait_recv()
 
     def product_only(i, carry):
         product_and_send(i)
@@ -432,17 +503,17 @@
 
     lax.fori_loop(early, chunks, both, 0)
 
+    def pass_chunk(i, carry):
+        pass_first_on(i)
+        return carry
+
+    lax.fori_loop(0, chunks, pass_chunk, 0)
+
     def first_wait(i, carry):
         for k in range(4):
-
-            @pl.when((r - steps[k] >= 0) & (r - steps[k] < blocks_n))
-            def _(k=k):
-                first_copy(i, k).wait_recv()
-
-            @pl.when((r + steps[k] >= 0) & (r + steps[k] < blocks_n))
-            def _(k=k):
-                first_copy(i, k).wait_send()
-
+            if k != 2:
+                guarded(receives(k), lambda k=k: first_copy(i, k).wait_recv())
+            guarded(sends(k), lambda k=k: first_copy(i, k).wait_send())
         return carry
 
     lax.fori_loop(0, chunks, first_wait, 0)
@@ -500,14 +571,17 @@
                 geo_copy(dq, c).wait_send()
 
     for c in range(2):
-        for dq in (-1, 0, 1):
-            for to in range(2):
-                if dq == 0 and to == c:
-                    continue
-
-                @pl.when((x == c) & inside(dq))
-                def _(c=c, dq=dq, to=to):
-                    sketch_copy(dq, c, to).wait_send()
+
+        @pl.when(x == c)
+        def _(c=c):
+            cross_copy(c).wait_send()
+
+        for dq in (-1, 1):
+
+            @pl.when((x == c) & inside(dq))
+            def _(c=c, dq=dq):
+                side_copy(dq, c, False).wait_send()
+                side_copy(dq, c, True).wait_send()
 
     pair.wait()
 
@@ -548,7 +622,7 @@
     wavenumber = 4.0 * math.sqrt(B)
     levels = 1 + rows_n.bit_length() - 1
     vmem = pl.BlockSpec(memory_space=pltpu.VMEM)
-    smem = pl.BlockSpec(memory_space=pltpu.SMEM)
+    hbm = pl.BlockSpec(memory_space=pltpu.HBM)
     gram, second = pl.pallas_call(
         functools.partial(fast_kernel, rows_n, wavenumber),
         name="sketch_twice",
@@ -556,7 +630,7 @@
             jax.ShapeDtypeStruct((128, 128), jnp.float32),
             jax.ShapeDtypeStruct((2 * B, 128), jnp.float32),
         ),
-        in_specs=[vmem, vmem, smem, smem],
+        in_specs=[hbm, hbm, hbm, hbm],
         out_specs=(vmem, vmem),
         scratch_shapes=[
             pltpu.VMEM((B, SLOTS * B), jnp.bfloat16),
@@ -574,6 +648,9 @@
             pltpu.SemaphoreType.DMA((2, 4, B // CHUNK)),
             pltpu.SemaphoreType.DMA((2, levels)),
             pltpu.SemaphoreType.DMA((2,)),
+            pltpu.SemaphoreType.DMA((4,)),
+            pltpu.SMEM((SLOTS, 2 * rows_n), jnp.int32),
+            pltpu.SMEM((2 * rows_n,), jnp.int32),
         ],
         compiler_params=pltpu.CompilerParams(
             collective_id=0, has_side_effects=True, vmem_limit_bytes=48 * 1024 * 1024

time: 74.9 us -> 72.6 us (0.969)
  Pallas kernels: 71.6 us -> 69.3 us
    pallas_call x1, Pallas kernels: 58.9 us -> 56.7 us  [fast_body(): pl.pallas_call(functools.partial(fast_kernel, rows_n, wavenumber), name='...]
where the time goes in v1:
time: 72.6 us; the launch traced here: 72.4 us
  Pallas kernels  69.3 us (95%)
  local copies, waits for them, and re-layouts  3.05 us (4%)
    pallas_call x1, Pallas kernels, fast_body(): pl.pallas_call(functools.partial(fast_kernel, rows_n, wavenumber), name='...  56.7 us
    pallas_call x1, Pallas kernels, fast_body(): pl.pallas_call(functools.partial(finish_kernel, scale), name='orthonormal...  12.7 us
    unnamed x8, local copies, waits for them, and re-layouts  3.05 us

profile of v1, /device:TPU:0, one launch (start us, length us, event | category | flops | bytes accessed | tf_op | source)
XLA Modules:
  0.0 72.4 jit_solution(4734039304945811700)
XLA Ops:
  0.0 0.0 copy-start.3
  0.0 0.7 copy-done.3
  0.7 0.0 copy-start
  0.7 0.9 %copy-done = bf16[64,2048]{1,0:T(8,128)(2,1)S(1)} copy-done((bf16[64,2048]{1,0:T(8,128)(2,1)S(1)}, bf16[64,2048]{1,0:T(8,128)(2,1)}, u32[]{:S(2)}) %copy-start) | copy-done | bytes 262168
  1.6 0.0 copy-start.1
  1.6 0.8 %copy-done.1 = f32[3,2048]{1,0:T(4,128)S(1)} copy-done((f32[3,2048]{1,0:T(4,128)S(1)}, f32[3,2048]{1,0:T(4,128)}, u32[]{:S(2)}) %copy-start.1) | copy-done | bytes 24600
  2.4 0.0 copy-start.2
  2.4 0.7 copy-done.2
  3.1 56.7 %sketch_twice.1 = (f32[128,128]{1,0:T(8,128)S(1)}, f32[2048,128]{1,0:T(8,128)S(1)}) custom-call(bf16[64,2048]{1,0:T(8,128)(2,1)S(1)} %copy-done, f32[3,2048]{1,0:T(4,128)S(1)} %copy-done.1, s32[5,32]{1,0:T(8,128)S(1)} %bitcast.1, s32[32]{0:T(128)S(1)} %copy-done.3), custom_call_target="tpu_custom_call" | custom-call | tf_op jit(solution)/shard_map/sketch_twice/pallas_call | solution.py:626
  59.7 12.7 %orthonormal_rows.1 = f32[64,2048]{1,0:T(8,128)} custom-call(f32[128,128]{1,0:T(8,128)S(1)} %get-tuple-element.7.gram, f32[2048,128]{1,0:T(8,128)S(1)} %get-tuple-element.8.second), custom_call_target="tpu_custom_call" | custom-call | tf_op jit(solution)/shard_map/orthonormal_rows/pallas_call | solution.py:660
Async XLA Ops:
  0.0 0.7 copy-start.3
  0.7 0.9 %copy-start = (bf16[64,2048]{1,0:T(8,128)(2,1)S(1)}, bf16[64,2048]{1,0:T(8,128)(2,1)}, u32[]{:S(2)}) copy-start(bf16[64,2048]{1,0:T(8,128)(2,1)} %sketch.1) | copy-start | bytes 786436
  1.6 0.8 %copy-start.1 = (f32[3,2048]{1,0:T(4,128)S(1)}, f32[3,2048]{1,0:T(4,128)}, u32[]{:S(2)}) copy-start(f32[3,2048]{1,0:T(4,128)} %geometry.1) | copy-start | bytes 73732
  2.4 0.7 copy-start.2

commit v2 on v1

--- a/solution.py
+++ b/solution.py
@@ -194,6 +194,7 @@
     own_x,
     own_y,
     own_a,
+    gram_sum,
     gram_send,
     gram_recv,
     geo_sem,
@@ -518,50 +519,56 @@
 
     lax.fori_loop(0, chunks, first_wait, 0)
 
+    def pair_copy(i):
+        rows = pl.ds(pl.multiple_of(x * B + i * CHUNK, CHUNK), CHUNK)
+        return pltpu.make_async_remote_copy(
+            src_ref=second.at[rows, :],
+            dst_ref=second.at[rows, :],
+            send_sem=pair_sem.at[0, i],
+            recv_sem=pair_sem.at[1, i],
+            device_id=(q, 1 - x),
+            device_id_type=MESH,
+        )
+
     def second_product(i, carry):
         at = pl.ds(pl.multiple_of(i * CHUNK, CHUNK), CHUNK)
         to = pl.ds(pl.multiple_of(x * B + i * CHUNK, CHUNK), CHUNK)
         part = jnp.dot(tiles[at, :], first[...], preferred_element_type=jnp.float32)
         second[to, :] = part
+        pair_copy(i).start()
         turned = jnp.transpose(part)
         product = jnp.dot(
             turned, part, precision=lax.Precision.HIGHEST, preferred_element_type=jnp.float32
         )
-        gram_send[0] += product
-        return carry
-
-    gram_send[0] = jnp.zeros((128, 128), jnp.float32)
+        gram_sum[...] += product
+        return carry
+
+    gram_sum[...] = jnp.zeros((128, 128), jnp.float32)
     lax.fori_loop(0, chunks, second_product, 0)
 
-    half = pl.ds(pl.multiple_of(x * B, B), B)
-    pair = pltpu.make_async_remote_copy(
-        src_ref=second.at[half, :],
-        dst_ref=second.at[half, :],
-        send_sem=pair_sem.at[0],
-        recv_sem=pair_sem.at[1],
-        device_id=(q, 1 - x),
-        device_id_type=MESH,
-    )
-
-    targets = [(q, 1 - x)] + [(partner_q(flip), x) for flip in flips]
-    for k, target in enumerate(targets):
+    def exchange(src, dst, k, target):
         copy = pltpu.make_async_remote_copy(
-            src_ref=gram_send.at[k],
-            dst_ref=gram_recv.at[k],
+            src_ref=src,
+            dst_ref=dst,
             send_sem=gram_sem.at[0, k],
             recv_sem=gram_sem.at[1, k],
             device_id=target,
             device_id_type=MESH,
         )
         copy.start()
-        if k == 0:
-            pair.start()
         copy.wait()
-        total = gram_send[k] + gram_recv[k]
-        if k + 1 < len(targets):
-            gram_send[k + 1] = total
-        else:
-            gram[...] = total
+
+    mine = pl.ds(pl.multiple_of((q % 2) * 64, 64), 64)
+    theirs = pl.ds(pl.multiple_of((1 - q % 2) * 64, 64), 64)
+    exchange(gram_sum.at[theirs, :], gram_recv.at[0], 0, (partner_q(1), x))
+    gram_send[0] = gram_sum[mine, :] + gram_recv[0]
+    targets = [(partner_q(flip), x) for flip in flips[1:]] + [(q, 1 - x)]
+    for k, target in enumerate(targets):
+        exchange(gram_send.at[k], gram_recv.at[k + 1], k + 1, target)
+        gram_send[k + 1] = gram_send[k] + gram_recv[k + 1]
+    last = len(targets)
+    gram[mine, :] = gram_send[last]
+    exchange(gram_send.at[last], gram.at[mine, :], last + 1, (partner_q(1), x))
 
     for c in range(2):
         for dq in (-1, 1):
@@ -583,7 +590,11 @@
                 side_copy(dq, c, False).wait_send()
                 side_copy(dq, c, True).wait_send()
 
-    pair.wait()
+    def pair_wait(i, carry):
+        pair_copy(i).wait()
+        return carry
+
+    lax.fori_loop(0, chunks, pair_wait, 0)
 
 
 def finish_kernel(scale, gram, second, modes, inverse):
@@ -641,13 +652,14 @@
             pltpu.VMEM((B, 128), jnp.float32),
             pltpu.VMEM((B, 128), jnp.float32),
             pltpu.VMEM((B, 128), jnp.float32),
-            pltpu.VMEM((levels, 128, 128), jnp.float32),
-            pltpu.VMEM((levels, 128, 128), jnp.float32),
+            pltpu.VMEM((128, 128), jnp.float32),
+            pltpu.VMEM((levels, 64, 128), jnp.float32),
+            pltpu.VMEM((levels, 64, 128), jnp.float32),
             pltpu.SemaphoreType.DMA((2, 2)),
             pltpu.SemaphoreType.DMA((2, 6)),
             pltpu.SemaphoreType.DMA((2, 4, B // CHUNK)),
-            pltpu.SemaphoreType.DMA((2, levels)),
-            pltpu.SemaphoreType.DMA((2,)),
+            pltpu.SemaphoreType.DMA((2, levels + 1)),
+            pltpu.SemaphoreType.DMA((2, B // CHUNK)),
             pltpu.SemaphoreType.DMA((4,)),
             pltpu.SMEM((SLOTS, 2 * rows_n), jnp.int32),
             pltpu.SMEM((2 * rows_n,), jnp.int32),
@@ -670,7 +682,7 @@
 
 def solution(mesh):
     rows_n, cols_n = mesh.shape["rows"], mesh.shape["cols"]
-    pair = cols_n == 2 and rows_n & (rows_n - 1) == 0
+    pair = cols_n == 2 and rows_n > 1 and rows_n & (rows_n - 1) == 0
     return jax.shard_map(
         fast_body if pair else body,
         mesh=mesh,

time: 72.6 us -> 70.9 us (0.977)
  Pallas kernels: 69.3 us -> 67.6 us
    pallas_call x1, Pallas kernels: 56.7 us -> 55 us  [fast_body(): pl.pallas_call(functools.partial(fast_kernel, rows_n, wavenumber), name='...]
where the time goes in v2:
time: 70.9 us; the launch traced here: 70.7 us
  Pallas kernels  67.6 us (95%)
  local copies, waits for them, and re-layouts  3.05 us (4%)
    pallas_call x1, Pallas kernels, fast_body(): pl.pallas_call(functools.partial(fast_kernel, rows_n, wavenumber), name='...  55 us
    pallas_call x1, Pallas kernels, fast_body(): pl.pallas_call(functools.partial(finish_kernel, scale), name='orthonormal...  12.6 us
    unnamed x8, local copies, waits for them, and re-layouts  3.05 us

profile of v2, /device:TPU:0, one launch (start us, length us, event | category | flops | bytes accessed | tf_op | source)
XLA Modules:
  0.0 70.7 jit_solution(1454972215125638318)
XLA Ops:
  0.0 0.0 copy-start.3
  0.0 0.7 copy-done.3
  0.7 0.0 copy-start
  0.7 0.9 %copy-done = bf16[64,2048]{1,0:T(8,128)(2,1)S(1)} copy-done((bf16[64,2048]{1,0:T(8,128)(2,1)S(1)}, bf16[64,2048]{1,0:T(8,128)(2,1)}, u32[]{:S(2)}) %copy-start) | copy-done | bytes 262168
  1.6 0.0 copy-start.1
  1.6 0.8 %copy-done.1 = f32[3,2048]{1,0:T(4,128)S(1)} copy-done((f32[3,2048]{1,0:T(4,128)S(1)}, f32[3,2048]{1,0:T(4,128)}, u32[]{:S(2)}) %copy-start.1) | copy-done | bytes 24600
  2.4 0.0 copy-start.2
  2.4 0.7 copy-done.2
  3.1 55.0 %sketch_twice.1 = (f32[128,128]{1,0:T(8,128)S(1)}, f32[2048,128]{1,0:T(8,128)S(1)}) custom-call(bf16[64,2048]{1,0:T(8,128)(2,1)S(1)} %copy-done, f32[3,2048]{1,0:T(4,128)S(1)} %copy-done.1, s32[5,32]{1,0:T(8,128)S(1)} %bitcast.1, s32[32]{0:T(128)S(1)} %copy-done.3), custom_call_target="tpu_custom_call" | custom-call | tf_op jit(solution)/shard_map/sketch_twice/pallas_call | solution.py:637
  58.0 12.6 %orthonormal_rows.1 = f32[64,2048]{1,0:T(8,128)} custom-call(f32[128,128]{1,0:T(8,128)S(1)} %get-tuple-element.7.gram, f32[2048,128]{1,0:T(8,128)S(1)} %get-tuple-element.8.second), custom_call_target="tpu_custom_call" | custom-call | tf_op jit(solution)/shard_map/orthonormal_rows/pallas_call | solution.py:672
Async XLA Ops:
  0.0 0.7 copy-start.3
  0.7 0.9 %copy-start = (bf16[64,2048]{1,0:T(8,128)(2,1)S(1)}, bf16[64,2048]{1,0:T(8,128)(2,1)}, u32[]{:S(2)}) copy-start(bf16[64,2048]{1,0:T(8,128)(2,1)} %sketch.1) | copy-start | bytes 786436
  1.6 0.8 %copy-start.1 = (f32[3,2048]{1,0:T(4,128)S(1)}, f32[3,2048]{1,0:T(4,128)}, u32[]{:S(2)}) copy-start(f32[3,2048]{1,0:T(4,128)} %geometry.1) | copy-start | bytes 73732
  2.4 0.7 copy-start.2

commit v3 on v2

--- a/solution.py
+++ b/solution.py
@@ -602,17 +602,42 @@
     lane = lax.broadcasted_iota(jnp.int32, (8, size), 1)
     sub = lax.broadcasted_iota(jnp.int32, (8, size), 0)
     groups = [gram[8 * k : 8 * k + 8, :] for k in range(size // 8)]
-    for j in range(size):
-        own, inner = j // 8, j % 8
-        line = groups[own][inner : inner + 1, :]
-        root = lax.rsqrt(line[:, j : j + 1])
-        line = jnp.where(lane[0:1] == j, 1.0, line) * root
-        for k in range(own, size // 8):
+    whole = (8, size)
+    for own in range(size // 8):
+        base = 8 * own
+        block = groups[own]
+        column = [jnp.broadcast_to(block[:, base + c : base + c + 1], whole) for c in range(8)]
+        roots, factor, lines = [], [], []
+        for p in range(8):
+            root = lax.rsqrt(jnp.broadcast_to(column[p][p : p + 1, :], whole))
+            scaled = column[p] * root
+            row = {}
+            for c in range(p + 1, 8):
+                row[c] = jnp.broadcast_to(column[c][p : p + 1, :], whole) * root
+                column[c] = column[c] - scaled * row[c]
+            line = jnp.broadcast_to(block[p : p + 1, :], whole)
+            line = jnp.where(lane == base + p, 1.0, line) * root
+            new = jnp.where(lane == base + p, 0.0, block) - scaled * line
+            block = jnp.where(sub > p, new, block)
+            roots.append(root)
+            factor.append(row)
+            lines.append(jnp.where((lane > base + p) & (lane < base + 8), 0.0, line))
+        result = lines[7]
+        for p in range(7):
+            result = jnp.where(sub == p, lines[p], result)
+        groups[own] = result
+        inside = (lane >= base) & (lane < base + 8)
+        for k in range(own + 1, size // 8):
             old = groups[k]
-            column = old[:, j : j + 1] * root
-            new = jnp.where(lane == j, 0.0, old) - column * line
-            if k == own:
-                new = jnp.where(sub > inner, new, jnp.where(sub == inner, line, old))
+            new = jnp.where(inside, 0.0, old)
+            parts = []
+            for p in range(8):
+                part = jnp.broadcast_to(old[:, base + p : base + p + 1], whole)
+                for before in range(p):
+                    part = part - parts[before] * factor[before][p]
+                part = part * roots[p]
+                parts.append(part)
+                new = new - part * lines[p]
             groups[k] = new
     for k in range(size // 8):
         inverse[8 * k : 8 * k + 8, :] = jnp.where(lane <= sub + 8 * k, groups[k], 0.0) * scale

time: 70.9 us -> 64.3 us (0.907)
  Pallas kernels: 67.6 us -> 60.9 us
    pallas_call x1, Pallas kernels: 12.6 us -> 5.98 us  [fast_body(): pl.pallas_call(functools.partial(finish_kernel, scale), name='orthonormal...]
where the time goes in v3:
time: 64.3 us; the launch traced here: 64 us
  Pallas kernels  60.9 us (95%)
  local copies, waits for them, and re-layouts  3.05 us (5%)
    pallas_call x1, Pallas kernels, fast_body(): pl.pallas_call(functools.partial(fast_kernel, rows_n, wavenumber), name='...  55 us
    pallas_call x1, Pallas kernels, fast_body(): pl.pallas_call(functools.partial(finish_kernel, scale), name='orthonormal...  5.98 us
    unnamed x8, local copies, waits for them, and re-layouts  3.05 us

profile of v3, /device:TPU:0, one launch (start us, length us, event | category | flops | bytes accessed | tf_op | source)
XLA Modules:
  0.0 64.0 jit_solution(10788908626364044635)
XLA Ops:
  0.0 0.0 copy-start.3
  0.0 0.7 %copy-done.3 = s32[32]{0:T(128)S(1)} copy-done((s32[32]{0:T(128)S(1)}, s32[32]{0:T(128)}, u32[]{:S(2)}) %copy-start.3) | copy-done | bytes 152
  0.7 0.0 copy-start
  0.7 0.9 %copy-done = bf16[64,2048]{1,0:T(8,128)(2,1)S(1)} copy-done((bf16[64,2048]{1,0:T(8,128)(2,1)S(1)}, bf16[64,2048]{1,0:T(8,128)(2,1)}, u32[]{:S(2)}) %copy-start) | copy-done | bytes 262168
  1.6 0.0 copy-start.1
  1.6 0.8 %copy-done.1 = f32[3,2048]{1,0:T(4,128)S(1)} copy-done((f32[3,2048]{1,0:T(4,128)S(1)}, f32[3,2048]{1,0:T(4,128)}, u32[]{:S(2)}) %copy-start.1) | copy-done | bytes 24600
  2.4 0.0 copy-start.2
  2.4 0.7 %copy-done.2 = s32[32,5]{0,1:T(8,128)S(1)} copy-done((s32[32,5]{0,1:T(8,128)S(1)}, s32[32,5]{0,1:T(8,128)}, u32[]{:S(2)}) %copy-start.2) | copy-done | bytes 664
  3.1 55.0 %sketch_twice.1 = (f32[128,128]{1,0:T(8,128)S(1)}, f32[2048,128]{1,0:T(8,128)S(1)}) custom-call(bf16[64,2048]{1,0:T(8,128)(2,1)S(1)} %copy-done, f32[3,2048]{1,0:T(4,128)S(1)} %copy-done.1, s32[5,32]{1,0:T(8,128)S(1)} %bitcast.1, s32[32]{0:T(128)S(1)} %copy-done.3), custom_call_target="tpu_custom_call" | custom-call | tf_op jit(solution)/shard_map/sketch_twice/pallas_call | solution.py:662
  58.0 6.0 %orthonormal_rows.1 = f32[64,2048]{1,0:T(8,128)} custom-call(f32[128,128]{1,0:T(8,128)S(1)} %get-tuple-element.7.gram, f32[2048,128]{1,0:T(8,128)S(1)} %get-tuple-element.8.second), custom_call_target="tpu_custom_call" | custom-call | tf_op jit(solution)/shard_map/orthonormal_rows/pallas_call | solution.py:697
Async XLA Ops:
  0.0 0.7 %copy-start.3 = (s32[32]{0:T(128)S(1)}, s32[32]{0:T(128)}, u32[]{:S(2)}) copy-start(s32[32]{0:T(128)} %counts_hbm.1) | copy-start | bytes 388
  0.7 0.9 %copy-start = (bf16[64,2048]{1,0:T(8,128)(2,1)S(1)}, bf16[64,2048]{1,0:T(8,128)(2,1)}, u32[]{:S(2)}) copy-start(bf16[64,2048]{1,0:T(8,128)(2,1)} %sketch.1) | copy-start | bytes 786436
  1.6 0.8 %copy-start.1 = (f32[3,2048]{1,0:T(4,128)S(1)}, f32[3,2048]{1,0:T(4,128)}, u32[]{:S(2)}) copy-start(f32[3,2048]{1,0:T(4,128)} %geometry.1) | copy-start | bytes 73732
  2.4 0.7 %copy-start.2 = (s32[32,5]{0,1:T(8,128)S(1)}, s32[32,5]{0,1:T(8,128)}, u32[]{:S(2)}) copy-start(s32[32,5]{0,1:T(8,128)} %param.6) | copy-start | bytes 1924

commit v4 on v3

--- a/solution.py
+++ b/solution.py
@@ -160,12 +160,11 @@
 CHUNK = 256
 GROUP = 256
 SIN = (
-    6.28318330620465,
-    -41.34144799998349,
-    81.59666336606338,
-    -76.58390226519525,
-    41.21913554078422,
-    -12.289783804974757,
+    6.2830557981504445,
+    -41.331214276596405,
+    81.36681478361689,
+    -74.47800141803688,
+    32.781394500276015,
 )
 MAGIC = 12582912.0
 
@@ -391,8 +390,8 @@
                     turns = square * inv
                     f = turns - ((turns + MAGIC) - MAGIC)
                     z = f * f
-                    poly = jnp.float32(SIN[5])
-                    for coefficient in SIN[4::-1]:
+                    poly = jnp.float32(SIN[4])
+                    for coefficient in SIN[3::-1]:
                         poly = poly * z + coefficient
                     value = (poly * f) * inv * (own_a[at, :] * col_a[:, part])
                     lanes = pl.ds(pl.multiple_of(g * width + lane * 128, 128), 128)

time: 64.3 us -> 63 us (0.980)
  Pallas kernels: 60.9 us -> 59.7 us
    pallas_call x1, Pallas kernels: 55 us -> 53.7 us  [fast_body(): pl.pallas_call(functools.partial(fast_kernel, rows_n, wavenumber), name='...]
where the time goes in v4:
time: 63 us; the launch traced here: 62.7 us
  Pallas kernels  59.7 us (95%)
  local copies, waits for them, and re-layouts  3.05 us (5%)
    pallas_call x1, Pallas kernels, fast_body(): pl.pallas_call(functools.partial(fast_kernel, rows_n, wavenumber), name='...  53.7 us
    pallas_call x1, Pallas kernels, fast_body(): pl.pallas_call(functools.partial(finish_kernel, scale), name='orthonormal...  5.98 us
    unnamed x8, local copies, waits for them, and re-layouts  3.05 us

profile of v4, /device:TPU:0, one launch (start us, length us, event | category | flops | bytes accessed | tf_op | source)
XLA Modules:
  0.0 62.7 jit_solution(3444935803416392313)
XLA Ops:
  0.0 0.0 copy-start.3
  0.0 0.7 %copy-done.3 = s32[32]{0:T(128)S(1)} copy-done((s32[32]{0:T(128)S(1)}, s32[32]{0:T(128)}, u32[]{:S(2)}) %copy-start.3) | copy-done | bytes 152
  0.7 0.0 copy-start
  0.7 0.9 %copy-done = bf16[64,2048]{1,0:T(8,128)(2,1)S(1)} copy-done((bf16[64,2048]{1,0:T(8,128)(2,1)S(1)}, bf16[64,2048]{1,0:T(8,128)(2,1)}, u32[]{:S(2)}) %copy-start) | copy-done | bytes 262168
  1.6 0.0 copy-start.1
  1.6 0.8 %copy-done.1 = f32[3,2048]{1,0:T(4,128)S(1)} copy-done((f32[3,2048]{1,0:T(4,128)S(1)}, f32[3,2048]{1,0:T(4,128)}, u32[]{:S(2)}) %copy-start.1) | copy-done | bytes 24600
  2.4 0.0 copy-start.2
  2.4 0.7 %copy-done.2 = s32[32,5]{0,1:T(8,128)S(1)} copy-done((s32[32,5]{0,1:T(8,128)S(1)}, s32[32,5]{0,1:T(8,128)}, u32[]{:S(2)}) %copy-start.2) | copy-done | bytes 664
  3.1 53.7 %sketch_twice.1 = (f32[128,128]{1,0:T(8,128)S(1)}, f32[2048,128]{1,0:T(8,128)S(1)}) custom-call(bf16[64,2048]{1,0:T(8,128)(2,1)S(1)} %copy-done, f32[3,2048]{1,0:T(4,128)S(1)} %copy-done.1, s32[5,32]{1,0:T(8,128)S(1)} %bitcast.1, s32[32]{0:T(128)S(1)} %copy-done.3), custom_call_target="tpu_custom_call" | custom-call | tf_op jit(solution)/shard_map/sketch_twice/pallas_call | solution.py:661
  56.8 6.0 %orthonormal_rows.1 = f32[64,2048]{1,0:T(8,128)} custom-call(f32[128,128]{1,0:T(8,128)S(1)} %get-tuple-element.7.gram, f32[2048,128]{1,0:T(8,128)S(1)} %get-tuple-element.8.second), custom_call_target="tpu_custom_call" | custom-call | tf_op jit(solution)/shard_map/orthonormal_rows/pallas_call | solution.py:696
Async XLA Ops:
  0.0 0.7 %copy-start.3 = (s32[32]{0:T(128)S(1)}, s32[32]{0:T(128)}, u32[]{:S(2)}) copy-start(s32[32]{0:T(128)} %counts_hbm.1) | copy-start | bytes 388
  0.7 0.9 %copy-start = (bf16[64,2048]{1,0:T(8,128)(2,1)S(1)}, bf16[64,2048]{1,0:T(8,128)(2,1)}, u32[]{:S(2)}) copy-start(bf16[64,2048]{1,0:T(8,128)(2,1)} %sketch.1) | copy-start | bytes 786436
  1.6 0.8 %copy-start.1 = (f32[3,2048]{1,0:T(4,128)S(1)}, f32[3,2048]{1,0:T(4,128)}, u32[]{:S(2)}) copy-start(f32[3,2048]{1,0:T(4,128)} %geometry.1) | copy-start | bytes 73732
  2.4 0.7 %copy-start.2 = (s32[32,5]{0,1:T(8,128)S(1)}, s32[32,5]{0,1:T(8,128)}, u32[]{:S(2)}) copy-start(s32[32,5]{0,1:T(8,128)} %param.6) | copy-start | bytes 1924
